TPU v7x, 128 devices: a whole 4x4x4 slice. The times are simulated.
128 devices in a mesh: seq: 8 (over z, core), tp: 16 (over x, y).
Axes of the slice: x: 4, y: 4, z: 4, core: 2. Of those that a mesh axis runs over, the one named last changes fastest.
Arguments:
- sequence_in: bfloat16 [1536, 4096], P('tp', 'seq')
- conv_weight: bfloat16 [3, 1536, 3, 1536], P(None, 'tp')
- norm_gain: float32 [3, 1536], P(None, 'tp'), may hold values from 0.1 to 1.9
- tissue_scale: float32 [367, 1536], replicated, may hold values from 0.3 to 3
- donor_offset: int32 [2048], P('seq'), may hold values from 0 to 511
- acceptor_owner: int32 [2048, 1], P('seq'), may hold values from 0 to 7; in each aligned block of 256 rows (0 to 255, 256 to 511, ...) at most 128 rows name the same one
- acceptor_offset: int32 [2048], P('seq'), may hold values from 0 to 511
- tissue: int32 [2048], P('seq'), may hold values from 0 to 366
- tower_grad: float32 [1536, 4096], P('tp', 'seq'), may hold values from -6 to 6
- score_grad: float32 [2048], P('seq'), may hold values from -24 to 24
Outputs:
- scores: float32 [2048], P('seq')
- input_grad: float32 [1536, 4096], P('tp', 'seq')
- weight_grad: float32 [3, 1536, 3, 1536], P(None, 'tp')
- gain_grad: float32 [3, 1536], P(None, 'tp')
Inputs may be any that keep to these rules, and one draw needn't show every extreme that they name: `acceptor_owner`: among the 256 junctions of one index of seq, at most 128 have their acceptor on one index of seq.
All inputs are finite; a program needn't handle non-finite values.
Results may differ from a plain program's by a relative error of at most 0.025.
Values may be sent and summed in bfloat16 or wider, within the bound.
A program may use at most 128 MiB of HBM per device.

v0:
```python
import math
import jax
import jax.numpy as jnp
from jax import lax
from jax.sharding import PartitionSpec as P

CHANNELS = 1536
LAYERS = 3
CAP = 128
EPSILON = 1e-06


def with_halo(x, sides, width):
    for axis, dim in sides:
        count, length = (lax.axis_size(axis), x.shape[dim])
        up = [(i, (i + 1) % count) for i in range(count - 1)]
        down = [(j, i) for i, j in up]
        last = lax.slice_in_dim(x, length - width, length, axis=dim)
        initial = lax.slice_in_dim(x, 0, width, axis=dim)
        before = lax.ppermute(last, axis, up)
        after = lax.ppermute(initial, axis, down)
        x = jnp.concatenate([before, x, after], axis=dim)
    return x


def gelu_fn(value):
    return jax.nn.gelu(value, approximate=True)


def widen(block, width):
    return with_halo(block, (("seq", 1),), width)


def forward_taps(weights, padded, reach, length):
    total = jnp.zeros((weights.shape[0], length), jnp.float32)
    for tap in range(3):
        total = total + jnp.dot(
            weights[:, tap, :],
            padded[:, tap * reach : tap * reach + length],
            preferred_element_type=jnp.float32,
        )
    return total


def backward_taps(weights, grad_pad, reach, length):
    total = jnp.zeros((weights.shape[2], length), jnp.float32)
    for tap in range(3):
        total = total + lax.dot_general(
            weights[:, tap, :],
            grad_pad[:, (2 - tap) * reach : (2 - tap) * reach + length],
            (((0,), (0,)), ((), ())),
            preferred_element_type=jnp.float32,
        )
    return total


def weight_taps(padded, grad_bf, reach, length):
    blocks = []
    for tap in range(3):
        blocks.append(
            lax.dot_general(
                grad_bf,
                padded[:, tap * reach : tap * reach + length],
                (((1,), (1,)), ((), ())),
                preferred_element_type=jnp.float32,
            )
        )
    return jnp.stack(blocks, axis=1)


def local(
    sequence_in,
    conv_weight,
    norm_gain,
    tissue_scale,
    donor_offset,
    acceptor_owner,
    acceptor_offset,
    tissue,
    tower_grad,
    score_grad,
):
    local_ch = sequence_in.shape[0]
    length = sequence_in.shape[1]
    seq_count = lax.axis_size("seq")
    state = sequence_in
    stored = []
    for layer in range(LAYERS):
        reach = 2 ** (layer + 3)
        stream = state.astype(jnp.float32)
        power = lax.psum(jnp.sum(stream * stream, axis=0), "tp") / CHANNELS
        inverse = 1.0 / jnp.sqrt(power + EPSILON)
        pre_act = stream * inverse[None, :] * norm_gain[layer][:, None]
        hidden = gelu_fn(pre_act).astype(jnp.bfloat16)
        padded = widen(hidden, reach)
        weights = conv_weight[layer]
        gathered = padded

        def fold_inputs(total, piece, start, weights=weights, reach=reach):
            return forward_taps(weights, piece, reach, length)

        mixed = fold_inputs(
            jnp.zeros((local_ch, length), jnp.float32),
            lax.all_gather(padded, "tp", axis=0, tiled=True),
            jnp.int32(0),
        )
        stored.append((state, inverse, pre_act, gathered))
        state = (stream + mixed).astype(jnp.bfloat16)
    owner = acceptor_owner[:, 0]
    member = (owner[:, None] == jnp.arange(seq_count, dtype=jnp.int32)[None, :]).astype(jnp.int32)
    slot = jnp.sum(jnp.cumsum(member, axis=0) * member, axis=1) - 1
    requests = jnp.zeros((seq_count, CAP), jnp.int32).at[owner, slot].set(acceptor_offset)
    rows_view = state.T
    offsets = lax.all_to_all(requests, "seq", split_axis=0, concat_axis=0, tiled=True)
    picked = rows_view[offsets]
    returned = lax.all_to_all(picked, "seq", split_axis=0, concat_axis=0, tiled=True)
    accept_cols = returned[owner, slot].astype(jnp.float32)
    donor_cols = rows_view[donor_offset].astype(jnp.float32)
    chan_start = lax.axis_index("tp") * local_ch
    local_table = lax.dynamic_slice_in_dim(tissue_scale, chan_start, local_ch, 1)
    tissue_hit = (
        tissue[:, None] == jnp.arange(tissue_scale.shape[0], dtype=jnp.int32)[None, :]
    ).astype(jnp.float32)
    tissue_rows = jnp.dot(tissue_hit, local_table, precision=lax.Precision.HIGHEST)
    root = math.sqrt(CHANNELS)
    partial_scores = jnp.sum(donor_cols * accept_cols * tissue_rows, axis=1) / root
    scores = lax.psum(partial_scores, "tp")
    weight_j = score_grad / root
    donor_back = weight_j[:, None] * accept_cols * tissue_rows
    accept_back = weight_j[:, None] * donor_cols * tissue_rows
    outgoing = jnp.zeros((seq_count, CAP, local_ch), jnp.float32).at[owner, slot].set(accept_back)
    incoming = lax.all_to_all(
        outgoing.astype(jnp.bfloat16), "seq", split_axis=0, concat_axis=0, tiled=True
    ).astype(outgoing.dtype)
    upstream = tower_grad.at[:, donor_offset].add(donor_back.T)
    upstream = upstream.at[:, offsets.reshape(-1)].add(incoming.reshape(-1, local_ch).T)
    weight_list = [None] * LAYERS
    gain_list = [None] * LAYERS
    for layer in reversed(range(LAYERS)):
        reach = 2 ** (layer + 3)
        old_state, inverse, pre_act, gathered = stored[layer]
        stream = old_state.astype(jnp.float32)
        grad_bf = upstream.astype(jnp.bfloat16)
        grad_pad = widen(grad_bf, reach)
        weights = conv_weight[layer]

        def term_rows(start, count, weights=weights, grad_pad=grad_pad, reach=reach):
            return backward_taps(weights, grad_pad, reach, length)

        back_hidden = lax.psum_scatter(
            term_rows(jnp.int32(0), local_ch * lax.axis_size("tp")).astype(jnp.bfloat16),
            "tp",
            scatter_dimension=0,
            tiled=True,
        ).astype(jnp.float32)

        def fold_weights(total, piece, start, grad_bf=grad_bf, reach=reach):
            return weight_taps(piece, grad_bf, reach, length)

        weight_term = fold_weights(
            jnp.zeros((local_ch, 3, CHANNELS), jnp.float32),
            lax.all_gather(gathered, "tp", axis=0, tiled=True),
            jnp.int32(0),
        )
        weight_list[layer] = lax.psum(weight_term.astype(jnp.bfloat16), "seq").astype(jnp.float32)
        _, gelu_back = jax.vjp(gelu_fn, pre_act)
        back_pre = gelu_back(back_hidden)[0]
        gain_list[layer] = jnp.sum(back_pre * stream * inverse[None, :], axis=1)
        back_norm = back_pre * norm_gain[layer][:, None]
        inner = lax.psum(jnp.sum(back_norm * stream, axis=0), "tp")
        upstream = (
            upstream
            + inverse[None, :] * back_norm
            - stream * (inverse**3)[None, :] * inner[None, :] / CHANNELS
        )
    gain_grad = lax.psum(jnp.stack(gain_list), "seq")
    return (scores, upstream, jnp.stack(weight_list), gain_grad)


def solution(mesh):
    return jax.shard_map(
        local,
        mesh=mesh,
        in_specs=(
            P("tp", "seq"),
            P(None, "tp", None, None),
            P(None, "tp"),
            P(),
            P("seq"),
            P("seq", None),
            P("seq"),
            P("seq"),
            P("tp", "seq"),
            P("seq"),
        ),
        out_specs=(P("seq"), P("tp", "seq"), P(None, "tp", None, None), P(None, "tp")),
        check_vma=False,
    )
```

profile of v0, /device:TPU:0, one launch (start us, length us, event | category | flops | bytes accessed | tf_op | source)
XLA Modules:
  0.0 813.4 jit_solution(14602728577334916671)
XLA Ops:
  9.6 40.8 %psum.77 = f32[512]{0:T(512)S(1)} all-reduce(f32[512]{0:T(512)S(1)} %fusion.133), channel_id=1, replica_groups=mesh['seq'=8,'tp'=16] {'tp'}, use_global_device_ids=true, to_apply=%region_1.0 | all-reduce | flops 512 | bytes 4096 | tf_op jit(solution)/shard_map/psum | solution.py:91
  54.7 3.9 collective-permute-done.1
  59.5 3.2 slice_bitcast_fusion
  62.6 40.5 %all-gather.4.cloned.1.call-done = bf16[1536,528]{1,0:T(8,128)(2,1)} async-done(((bf16[96,528]{1,0:T(8,128)(2,1)}), bf16[1536,528]{1,0:T(8,128)(2,1)}) %all-gather.4.cloned.1.call-update) | async-done | bytes 1622032 | tf_op jit(solution)/shard_map/all_gather | solution.py:104
  108.2 38.1 %psum.78 = f32[512]{0:T(512)S(1)} all-reduce(f32[512]{0:T(512)S(1)} %get-tuple-element.50), channel_id=1, replica_groups=mesh['seq'=8,'tp'=16] {'tp'}, use_global_device_ids=true, to_apply=%region_3.0 | all-reduce | flops 512 | bytes 4096 | tf_op jit(solution)/shard_map/psum | solution.py:91
  149.7 3.6 collective-permute-done.3
  154.1 42.9 %all-gather.6.cloned.1.call-done = bf16[1536,544]{1,0:T(8,128)(2,1)} async-done(((bf16[96,544]{1,0:T(8,128)(2,1)}), bf16[1536,544]{1,0:T(8,128)(2,1)}) %all-gather.6.cloned.1.call-update) | async-done | bytes 1671184 | tf_op jit(solution)/shard_map/all_gather | solution.py:104
  200.5 38.3 %psum.79 = f32[512]{0:T(512)S(1)} all-reduce(f32[512]{0:T(512)S(1)} %get-tuple-element.52), channel_id=1, replica_groups=mesh['seq'=8,'tp'=16] {'tp'}, use_global_device_ids=true, to_apply=%region_5.0 | all-reduce | flops 512 | bytes 4096 | tf_op jit(solution)/shard_map/psum | solution.py:91
  242.9 3.6 collective-permute-done.5
  248.8 38.6 %scatter_fusion = s32[8,128]{1,0:T(8,128)} fusion(s32[8,128]{1,0:T(8,128)} %broadcast.150, s32[256]{0:T(256)S(1)} %bitcast.150, s32[256]{0:T(256)} %param.16), kind=kCustom, calls=%fused_computation.3 | custom fusion | bytes 5120 | tf_op jit(solution)/shard_map/scatter | solution.py:112
  287.5 6.3 all-to-all-start
  294.4 4.6 all-to-all-done
  304.2 3.2 gather_fusion.1
  308.3 3.4 all-to-all-start.1
  312.7 5.7 all-to-all-done.1
  322.2 16.8 %scatter_fusion.2 = f32[8,128,96]{2,1,0:T(8,128)S(1)} fusion(f32[8,128,96]{2,1,0:T(8,128)S(1)} %broadcast_in_dim.5, s32[256]{0:T(256)S(1)} %bitcast.151, f32[256,96]{1,0:T(8,128)} %copy.100), kind=kCustom, calls=%fused_computation.5 | custom fusion | bytes 296960 | tf_op jit(solution)/shard_map/scatter | solution.py:131
  339.8 4.0 all-to-all-start.2
  346.4 4.3 all-to-all-done.2
  351.7 6.3 scatter_fusion.3
  358.1 2.7 collective-permute-start.7
  368.0 71.8 %reduce-scatter.4.cloned.1.call-done = bf16[96,512]{1,0:T(8,128)(2,1)} async-done(((bf16[1536,512]{1,0:T(8,128)(2,1)}), bf16[96,512]{1,0:T(8,128)(2,1)}) %reduce-scatter.4.cloned.1.call-update) | async-done | bytes 98320 | tf_op jit(solution)/shard_map/reduce_scatter | solution.py:150
  441.0 38.1 %psum.81 = f32[512]{0:T(512)S(1)} all-reduce(f32[512]{0:T(512)S(1)} %get-tuple-element.7), channel_id=1, replica_groups=mesh['seq'=8,'tp'=16] {'tp'}, use_global_device_ids=true, to_apply=%region_17.18 | all-reduce | flops 512 | bytes 4096 | tf_op jit(solution)/shard_map/psum | solution.py:170
  486.1 2.9 collective-permute-done.8
  490.9 2.6 fusion.16
  499.2 64.4 %reduce-scatter.6.cloned.1.call-done = bf16[96,512]{1,0:T(8,128)(2,1)} async-done(((bf16[1536,512]{1,0:T(8,128)(2,1)}), bf16[96,512]{1,0:T(8,128)(2,1)}) %reduce-scatter.6.cloned.1.call-update) | async-done | bytes 98320 | tf_op jit(solution)/shard_map/reduce_scatter | solution.py:150
  564.9 38.3 %psum.82 = f32[512]{0:T(512)S(1)} all-reduce(f32[512]{0:T(512)S(1)} %get-tuple-element.5), channel_id=1, replica_groups=mesh['seq'=8,'tp'=16] {'tp'}, use_global_device_ids=true, to_apply=%region_20.21 | all-reduce | flops 512 | bytes 4096 | tf_op jit(solution)/shard_map/psum | solution.py:170
  613.4 2.9 collective-permute-done.10
  618.1 55.7 %all-reduce.4.cloned.1.call-done = (bf16[1,96,3,1536]{3,1,2,0:T(8,128)(2,1)}, bf16[1,96,3,1536]{3,1,2,0:T(8,128)(2,1)}, bf16[1,96,3,1536]{3,1,2,0:T(8,128)(2,1)}) async-done(((bf16[1,96,3,1536]{3,1,2,0:T(8,128)(2,1)}, bf16[1,96,3,1536]{3,1,2,0:T(8,128)(2,1)}, bf16[1,96,3,1536]{3,1,2,0:T(8,128)(2,1)}), (bf16[1,96,3,1536]{3,1,2,0:T(8,128)(2,1)}, bf16[1,96,3,1536]{3,1,2,0:T(8,128)(2,1)}, ...) | async-done | bytes 2654224 | tf_op jit(solution)/shard_map/psum | solution.py:165
  673.8 4.5 maximum_convert_fusion
  678.3 72.7 %reduce-scatter.8.cloned.1.call-done = bf16[96,512]{1,0:T(8,128)(2,1)} async-done(((bf16[1536,512]{1,0:T(8,128)(2,1)}), bf16[96,512]{1,0:T(8,128)(2,1)}) %reduce-scatter.8.cloned.1.call-update) | async-done | bytes 98320 | tf_op jit(solution)/shard_map/reduce_scatter | solution.py:150
  752.3 13.7 %psum.87 = f32[3,96]{1,0:T(4,128)} all-reduce(f32[3,96]{1,0:T(4,128)S(1)} %pad_maximum_fusion.15), channel_id=1, replica_groups=mesh['seq'=8,'tp'=16] {'seq'}, use_global_device_ids=true, to_apply=%region_30.31 | all-reduce | flops 288 | bytes 2304 | tf_op jit(solution)/shard_map/psum | solution.py:176
  766.1 38.6 %all-reduce = (f32[256]{0:T(256)}, f32[512]{0:T(512)S(1)}) all-reduce(f32[256]{0:T(256)S(1)} %broadcast_multiply_fusion.1, f32[512]{0:T(512)S(1)} %get-tuple-element.9), channel_id=1, replica_groups=mesh['seq'=8,'tp'=16] {'tp'}, use_global_device_ids=true, to_apply=%region_11.12 | all-reduce | flops 768 | bytes 6144 | tf_op jit(solution)/shard_map/psum | solution.py:127
  (184 shorter events, 81.3 us)
Async XLA Ops:
  7.2 313.2 %copy-start = (f32[367,1536]{1,0:T(8,128)S(1)}, f32[367,1536]{1,0:T(8,128)}, u32[]{:S(2)}) copy-start(f32[367,1536]{1,0:T(8,128)} %param.13) | copy-start | bytes 6764548
  7.2 96.0 %all-gather.4.cloned.1.call-start = ((), (), s32[]{:S(2)}) async-start(), calls=%async_computation.6 | async-start | bytes 2088960 | tf_op jit(solution)/shard_map/all_gather | solution.py:104
  8.7 138.3 %copy-start.24 = (f32[96]{0:T(128)}, f32[96]{0:T(128)S(1)}, u32[]{:S(2)}) copy-start(f32[96]{0:T(128)S(1)} %get-tuple-element.47) | copy-start | bytes 1156
  52.1 2.6 collective-permute-start
  53.4 5.2 collective-permute-start.1
  59.4 137.7 %all-gather.6.cloned.1.call-start = ((), (), s32[]{:S(2)}) async-start(), calls=%async_computation.7 | async-start | bytes 2088960 | tf_op jit(solution)/shard_map/all_gather | solution.py:104
  62.6 137.5 %copy-start.1 = (bf16[96,3,1536]{2,0,1:T(8,128)(2,1)}, bf16[96,3,1536]{2,0,1:T(8,128)(2,1)S(1)}, u32[]{:S(2)}) copy-start(bf16[96,3,1536]{2,0,1:T(8,128)(2,1)S(1)} %get-tuple-element.23) | copy-start | bytes 2654212
  147.1 2.6 collective-permute-start.2
  148.4 4.9 collective-permute-start.3
  154.1 145.0 %all-gather.8.cloned.1.call-start = ((), (), s32[]{:S(2)}) async-start(), calls=%async_computation.8 | async-start | bytes 2088960 | tf_op jit(solution)/shard_map/all_gather | solution.py:104
  200.5 93.3 %copy-start.29 = (s32[256]{0:T(256)S(1)}, s32[256]{0:T(256)}, u32[]{:S(2)}) copy-start(s32[256]{0:T(256)} %param.14) | copy-start | bytes 3076
  200.5 93.8 %copy-start.14 = (f32[96,512]{1,0:T(8,128)S(1)}, f32[96,512]{1,0:T(8,128)}, u32[]{:S(2)}) copy-start(f32[96,512]{1,0:T(8,128)} %param.18) | copy-start | bytes 589828
  240.3 2.6 collective-permute-start.4
  241.6 4.9 collective-permute-start.5
  287.5 11.6 %all-to-all-start = ((s32[8,1,128]{2,1,0:T(1,128)}), s32[8,1,128]{2,1,0:T(1,128)S(1)}, u32[]{:S(2)}, u32[]{:S(2)}) async-start(s32[8,1,128]{2,1,0:T(1,128)} %bitcast.27), calls=%async_computation | async-start | bytes 8192 | tf_op jit(solution)/shard_map/all_to_all | solution.py:114
  308.3 10.1 %all-to-all-start.1 = ((bf16[8,128,96]{1,2,0:T(8,128)(2,1)}), bf16[8,128,96]{1,2,0:T(8,128)(2,1)S(1)}, u32[]{:S(2)}, u32[]{:S(2)}) async-start(bf16[8,128,96]{1,2,0:T(8,128)(2,1)} %copy.95), calls=%async_computation.1 | async-start | bytes 393216 | tf_op jit(solution)/shard_map/all_to_all | solution.py:116
  339.8 10.8 %all-to-all-start.2 = ((bf16[8,128,96]{1,2,0:T(8,128)(2,1)}), bf16[8,128,96]{1,2,0:T(8,128)(2,1)}, u32[]{:S(2)}, u32[]{:S(2)}) async-start(bf16[8,128,96]{1,2,0:T(8,128)(2,1)} %copy.101), calls=%async_computation.2 | async-start | bytes 393216 | tf_op jit(solution)/shard_map/all_to_all | solution.py:132
  343.9 95.9 %reduce-scatter.4.cloned.1.call-start = ((), (), s32[]{:S(2)}) async-start(), calls=%async_computation.9 | async-start | bytes 1671168 | tf_op jit(solution)/shard_map/reduce_scatter | solution.py:150
  358.1 5.6 collective-permute-start.7
  362.4 3.6 collective-permute-start.6
  367.8 111.4 %copy-start.21 = (f32[512]{0:T(512)S(1)}, f32[512]{0:T(512)}, u32[]{:S(2)}) copy-start(f32[512]{0:T(512)} %get-tuple-element.43) | copy-start | bytes 6148
  367.8 195.9 %reduce-scatter.6.cloned.1.call-start = ((), (), s32[]{:S(2)}) async-start(), calls=%async_computation.10 | async-start | bytes 1671168 | tf_op jit(solution)/shard_map/reduce_scatter | solution.py:150
  481.1 4.3 collective-permute-start.9
  484.1 4.9 collective-permute-start.8
  490.8 183.0 %all-reduce.4.cloned.1.call-start = ((), (), s32[]{:S(2)}) async-start(), calls=%async_computation.12 | async-start | bytes 5308416 | tf_op jit(solution)/shard_map/psum | solution.py:165
  497.4 105.9 %copy-start.13 = (f32[96,512]{1,0:T(8,128)S(1)}, f32[96,512]{1,0:T(8,128)}, u32[]{:S(2)}) copy-start(f32[96,512]{1,0:T(8,128)} %get-tuple-element.18) | copy-start | bytes 589828
  497.4 105.9 %copy-start.20 = (f32[512]{0:T(512)S(1)}, f32[512]{0:T(512)}, u32[]{:S(2)}) copy-start(f32[512]{0:T(512)} %get-tuple-element.41) | copy-start | bytes 6148
  609.3 141.7 %reduce-scatter.8.cloned.1.call-start = ((), (), s32[]{:S(2)}) async-start(), calls=%async_computation.11 | async-start | bytes 1671168 | tf_op jit(solution)/shard_map/reduce_scatter | solution.py:150
  609.5 3.2 collective-permute-start.11
  611.4 4.9 collective-permute-start.10
  673.8 77.3 %copy-start.23 = (f32[96]{0:T(128)S(1)}, f32[96]{0:T(128)}, u32[]{:S(2)}) copy-start(f32[96]{0:T(128)} %copy-done.22) | copy-start | bytes 1156
  673.8 130.9 %copy-start.19 = (f32[512]{0:T(512)S(1)}, f32[512]{0:T(512)}, u32[]{:S(2)}) copy-start(f32[512]{0:T(512)} %get-tuple-element.39) | copy-start | bytes 6148
  (23 other events, 464.0 us)
Sparse Core Ops, SparseCore 0:
  59.5 43.5 all-gather.3
  154.2 42.8 all-gather.5
  247.4 42.8 all-gather.7
  367.9 71.7 reduce-scatter.3
  490.9 72.7 reduce-scatter.5
  609.5 64.2 all-reduce.3
  677.0 73.9 reduce-scatter.7
where the time goes:
time: 816 us; the launch traced here: 813 us
  waiting for transfers between devices  381 us (47%)
  blocking collectives  246 us (30%)
  local copies, waits for them, and re-layouts  71.9 us (9%)
  matrix products  35.4 us (4%)
  other arithmetic  32.8 us (4%)
  starting transfers between devices  30.9 us (4%)
  between operations  14.9 us (2%)
    reduce_scatter x3, waiting for transfers between devices, local(): lax.psum_scatter(term_rows(jnp.int32(0), local_ch * lax.axis_size('tp'))....  209 us
    psum x3, blocking collectives, local(): power = lax.psum(jnp.sum(stream * stream, axis=0), 'tp') / CHANNELS  117 us
    all_gather x3, waiting for transfers between devices, local(): lax.all_gather(padded, 'tp', axis=0, tiled=True)  83.4 us
    psum x2, blocking collectives, local(): inner = lax.psum(jnp.sum(back_norm * stream, axis=0), 'tp')  76.5 us
    psum x1, waiting for transfers between devices, local(): lax.psum(weight_term.astype(jnp.bfloat16), 'seq').astype(jnp.float32)  55.7 us
    psum x1, blocking collectives, local(): scores = lax.psum(partial_scores, 'tp')  38.6 us
    scatter x1, local copies, waits for them, and re-layouts, local(): jnp.zeros((seq_count, CAP), jnp.int32).at[owner, slot].set(acceptor_offset)  38.6 us
    ppermute x6, waiting for transfers between devices, with_halo(): after = lax.ppermute(initial, axis, down)  18.6 us
  transfers between devices with their start and end apart: 22, of which 15 were waited for; matrix products, arithmetic and copies ran while one was open for 8% of the time, Pallas kernels for 0%

commit v1 on v0

--- a/solution.py
+++ b/solution.py
@@ -124,7 +124,8 @@
     tissue_rows = jnp.dot(tissue_hit, local_table, precision=lax.Precision.HIGHEST)
     root = math.sqrt(CHANNELS)
     partial_scores = jnp.sum(donor_cols * accept_cols * tissue_rows, axis=1) / root
-    scores = lax.psum(partial_scores, "tp")
+    pieces = lax.all_gather(partial_scores, "tp")
+    scores = jnp.sum(pieces, axis=0)
     weight_j = score_grad / root
     donor_back = weight_j[:, None] * accept_cols * tissue_rows
     accept_back = weight_j[:, None] * donor_cols * tissue_rows

time: 816 us -> 817 us (level)
  waiting for transfers between devices: 381 us -> 361 us
  blocking collectives: 246 us -> 265 us
    psum x1 -> x0, blocking collectives: 38.6 us -> none  [local(): scores = lax.psum(partial_scores, 'tp')]
    psum x2 -> x3, blocking collectives: 76.5 us -> 115 us  [local(): inner = lax.psum(jnp.sum(back_norm * stream, axis=0), 'tp')]
    psum x1, waiting for transfers between devices: 55.7 us -> 35.1 us  [local(): lax.psum(weight_term.astype(jnp.bfloat16), 'seq').astype(jnp.float32)]
    all_gather x0 -> x1, blocking collectives: none -> 20.1 us  [local(): pieces = lax.all_gather(partial_scores, 'tp')]
where the time goes in v1:
time: 817 us; the launch traced here: 814 us
  waiting for transfers between devices  361 us (44%)
  blocking collectives  265 us (32%)
  local copies, waits for them, and re-layouts  71.1 us (9%)
  matrix products  35.4 us (4%)
  other arithmetic  34.6 us (4%)
  starting transfers between devices  30.9 us (4%)
  between operations  15 us (2%)
    reduce_scatter x3, waiting for transfers between devices, local(): lax.psum_scatter(term_rows(jnp.int32(0), local_ch * lax.axis_size('tp'))....  209 us
    psum x3, blocking collectives, local(): power = lax.psum(jnp.sum(stream * stream, axis=0), 'tp') / CHANNELS  117 us
    psum x3, blocking collectives, local(): inner = lax.psum(jnp.sum(back_norm * stream, axis=0), 'tp')  115 us
    all_gather x3, waiting for transfers between devices, local(): lax.all_gather(padded, 'tp', axis=0, tiled=True)  83.4 us
    scatter x1, local copies, waits for them, and re-layouts, local(): jnp.zeros((seq_count, CAP), jnp.int32).at[owner, slot].set(acceptor_offset)  38.4 us
    psum x1, waiting for transfers between devices, local(): lax.psum(weight_term.astype(jnp.bfloat16), 'seq').astype(jnp.float32)  35.1 us
    all_gather x1, blocking collectives, local(): pieces = lax.all_gather(partial_scores, 'tp')  20.1 us
    ppermute x6, waiting for transfers between devices, with_halo(): after = lax.ppermute(initial, axis, down)  18.6 us
  transfers between devices with their start and end apart: 22, of which 15 were waited for; matrix products, arithmetic and copies ran while one was open for 8% of the time, Pallas kernels for 0%

profile of v1, /device:TPU:0, one launch (start us, length us, event | category | flops | bytes accessed | tf_op | source)
XLA Modules:
  0.0 813.8 jit_solution(3684337275662829531)
XLA Ops:
  9.6 40.8 %psum.70 = f32[512]{0:T(512)S(1)} all-reduce(f32[512]{0:T(512)S(1)} %fusion.133), channel_id=1, replica_groups=mesh['seq'=8,'tp'=16] {'tp'}, use_global_device_ids=true, to_apply=%region_1.0 | all-reduce | flops 512 | bytes 4096 | tf_op jit(solution)/shard_map/psum | solution.py:91
  54.7 3.9 collective-permute-done.1
  59.5 3.2 slice_bitcast_fusion
  62.6 40.5 %all-gather.6.cloned.1.call-done = bf16[1536,528]{1,0:T(8,128)(2,1)} async-done(((bf16[96,528]{1,0:T(8,128)(2,1)}), bf16[1536,528]{1,0:T(8,128)(2,1)}) %all-gather.6.cloned.1.call-update) | async-done | bytes 1622032 | tf_op jit(solution)/shard_map/all_gather | solution.py:104
  108.2 38.1 %psum.71 = f32[512]{0:T(512)S(1)} all-reduce(f32[512]{0:T(512)S(1)} %get-tuple-element.48), channel_id=1, replica_groups=mesh['seq'=8,'tp'=16] {'tp'}, use_global_device_ids=true, to_apply=%region_3.0 | all-reduce | flops 512 | bytes 4096 | tf_op jit(solution)/shard_map/psum | solution.py:91
  149.7 3.6 collective-permute-done.3
  154.1 42.9 %all-gather.8.cloned.1.call-done = bf16[1536,544]{1,0:T(8,128)(2,1)} async-done(((bf16[96,544]{1,0:T(8,128)(2,1)}), bf16[1536,544]{1,0:T(8,128)(2,1)}) %all-gather.8.cloned.1.call-update) | async-done | bytes 1671184 | tf_op jit(solution)/shard_map/all_gather | solution.py:104
  200.5 38.3 %psum.72 = f32[512]{0:T(512)S(1)} all-reduce(f32[512]{0:T(512)S(1)} %get-tuple-element.50), channel_id=1, replica_groups=mesh['seq'=8,'tp'=16] {'tp'}, use_global_device_ids=true, to_apply=%region_5.0 | all-reduce | flops 512 | bytes 4096 | tf_op jit(solution)/shard_map/psum | solution.py:91
  242.9 3.6 collective-permute-done.5
  248.8 38.4 %scatter_fusion = s32[8,128]{1,0:T(8,128)} fusion(s32[8,128]{1,0:T(8,128)} %broadcast.159, s32[256]{0:T(256)S(1)} %bitcast.151, s32[256]{0:T(256)} %param.16), kind=kCustom, calls=%fused_computation.3 | custom fusion | bytes 5120 | tf_op jit(solution)/shard_map/scatter | solution.py:112
  287.1 6.3 all-to-all-start
  293.6 5.1 all-to-all-done
  303.9 3.2 gather_fusion.1
  308.0 3.4 all-to-all-start.1
  312.4 5.7 all-to-all-done.1
  321.9 16.8 %scatter_fusion.2 = f32[8,128,96]{2,1,0:T(8,128)S(1)} fusion(f32[8,128,96]{2,1,0:T(8,128)S(1)} %broadcast_in_dim.5, s32[256]{0:T(256)S(1)} %bitcast.152, f32[256,96]{1,0:T(8,128)} %copy.100), kind=kCustom, calls=%fused_computation.5 | custom fusion | bytes 296960 | tf_op jit(solution)/shard_map/scatter | solution.py:132
  339.5 4.0 all-to-all-start.2
  346.1 4.3 all-to-all-done.2
  351.4 6.3 scatter_fusion.3
  357.8 2.7 collective-permute-start.7
  367.7 71.6 %reduce-scatter.4.cloned.1.call-done = bf16[96,512]{1,0:T(8,128)(2,1)} async-done(((bf16[1536,512]{1,0:T(8,128)(2,1)}), bf16[96,512]{1,0:T(8,128)(2,1)}) %reduce-scatter.4.cloned.1.call-update) | async-done | bytes 98320 | tf_op jit(solution)/shard_map/reduce_scatter | solution.py:151
  441.2 38.1 %psum.73 = f32[512]{0:T(512)S(1)} all-reduce(f32[512]{0:T(512)S(1)} %get-tuple-element.7), channel_id=1, replica_groups=mesh['seq'=8,'tp'=16] {'tp'}, use_global_device_ids=true, to_apply=%region_17.18 | all-reduce | flops 512 | bytes 4096 | tf_op jit(solution)/shard_map/psum | solution.py:171
  485.5 2.9 collective-permute-done.8
  498.7 64.6 %reduce-scatter.6.cloned.1.call-done = bf16[96,512]{1,0:T(8,128)(2,1)} async-done(((bf16[1536,512]{1,0:T(8,128)(2,1)}), bf16[96,512]{1,0:T(8,128)(2,1)}) %reduce-scatter.6.cloned.1.call-update) | async-done | bytes 98320 | tf_op jit(solution)/shard_map/reduce_scatter | solution.py:151
  565.1 38.3 %psum.74 = f32[512]{0:T(512)S(1)} all-reduce(f32[512]{0:T(512)S(1)} %get-tuple-element.5), channel_id=1, replica_groups=mesh['seq'=8,'tp'=16] {'tp'}, use_global_device_ids=true, to_apply=%region_20.21 | all-reduce | flops 512 | bytes 4096 | tf_op jit(solution)/shard_map/psum | solution.py:171
  614.2 2.9 collective-permute-done.10
  618.9 20.1 %all-gather.1 = f32[16,1,256]{2,1,0:T(1,128)S(1)} all-gather(f32[1,1,256]{2,1,0:T(1,128)S(1)} %bitcast.162), channel_id=2, replica_groups=mesh['seq'=8,'tp'=16] {'tp'}, dimensions={0}, use_global_device_ids=true | all-gather | bytes 17408 | tf_op jit(solution)/shard_map/all_gather | solution.py:127
  639.6 35.1 %all-reduce.3.cloned.1.call-done = (bf16[1,96,3,1536]{3,1,2,0:T(8,128)(2,1)}, bf16[1,96,3,1536]{3,1,2,0:T(8,128)(2,1)}, bf16[1,96,3,1536]{3,1,2,0:T(8,128)(2,1)}) async-done(((bf16[1,96,3,1536]{3,1,2,0:T(8,128)(2,1)}, bf16[1,96,3,1536]{3,1,2,0:T(8,128)(2,1)}, bf16[1,96,3,1536]{3,1,2,0:T(8,128)(2,1)}), (bf16[1,96,3,1536]{3,1,2,0:T(8,128)(2,1)}, bf16[1,96,3,1536]{3,1,2,0:T(8,128)(2,1)}, ...) | async-done | bytes 2654224 | tf_op jit(solution)/shard_map/psum | solution.py:166
  674.7 4.5 maximum_convert_fusion
  679.2 72.7 %reduce-scatter.8.cloned.1.call-done = bf16[96,512]{1,0:T(8,128)(2,1)} async-done(((bf16[1536,512]{1,0:T(8,128)(2,1)}), bf16[96,512]{1,0:T(8,128)(2,1)}) %reduce-scatter.8.cloned.1.call-update) | async-done | bytes 98320 | tf_op jit(solution)/shard_map/reduce_scatter | solution.py:151
  753.2 13.7 %psum.79 = f32[3,96]{1,0:T(4,128)} all-reduce(f32[3,96]{1,0:T(4,128)S(1)} %pad_maximum_fusion.15), channel_id=1, replica_groups=mesh['seq'=8,'tp'=16] {'seq'}, use_global_device_ids=true, to_apply=%region_30.31 | all-reduce | flops 288 | bytes 2304 | tf_op jit(solution)/shard_map/psum | solution.py:177
  767.0 38.1 %psum.75 = f32[512]{0:T(512)S(1)} all-reduce(f32[512]{0:T(512)S(1)} %get-tuple-element.9), channel_id=1, replica_groups=mesh['seq'=8,'tp'=16] {'tp'}, use_global_device_ids=true, to_apply=%region_23.24 | all-reduce | flops 512 | bytes 4096 | tf_op jit(solution)/shard_map/psum | solution.py:171
  (190 shorter events, 85.1 us)
Async XLA Ops:
  7.2 312.9 %copy-start = (f32[367,1536]{1,0:T(8,128)S(1)}, f32[367,1536]{1,0:T(8,128)}, u32[]{:S(2)}) copy-start(f32[367,1536]{1,0:T(8,128)} %param.13) | copy-start | bytes 6764548
  7.2 95.9 %all-gather.6.cloned.1.call-start = ((), (), s32[]{:S(2)}) async-start(), calls=%async_computation.6 | async-start | bytes 2088960 | tf_op jit(solution)/shard_map/all_gather | solution.py:104
  8.7 138.2 %copy-start.24 = (f32[96]{0:T(128)}, f32[96]{0:T(128)S(1)}, u32[]{:S(2)}) copy-start(f32[96]{0:T(128)S(1)} %get-tuple-element.45) | copy-start | bytes 1156
  52.1 2.6 collective-permute-start
  53.4 5.2 collective-permute-start.1
  59.4 137.7 %all-gather.8.cloned.1.call-start = ((), (), s32[]{:S(2)}) async-start(), calls=%async_computation.7 | async-start | bytes 2088960 | tf_op jit(solution)/shard_map/all_gather | solution.py:104
  62.6 137.4 %copy-start.1 = (bf16[96,3,1536]{2,0,1:T(8,128)(2,1)}, bf16[96,3,1536]{2,0,1:T(8,128)(2,1)S(1)}, u32[]{:S(2)}) copy-start(bf16[96,3,1536]{2,0,1:T(8,128)(2,1)S(1)} %get-tuple-element.21) | copy-start | bytes 2654212
  147.1 2.6 collective-permute-start.2
  148.4 4.9 collective-permute-start.3
  154.1 144.6 %all-gather.10.cloned.1.call-start = ((), (), s32[]{:S(2)}) async-start(), calls=%async_computation.8 | async-start | bytes 2088960 | tf_op jit(solution)/shard_map/all_gather | solution.py:104
  200.5 92.9 %copy-start.31 = (s32[256]{0:T(256)S(1)}, s32[256]{0:T(256)}, u32[]{:S(2)}) copy-start(s32[256]{0:T(256)} %param.14) | copy-start | bytes 3076
  200.5 93.0 %copy-start.14 = (f32[96,512]{1,0:T(8,128)S(1)}, f32[96,512]{1,0:T(8,128)}, u32[]{:S(2)}) copy-start(f32[96,512]{1,0:T(8,128)} %param.18) | copy-start | bytes 589828
  240.3 2.6 collective-permute-start.4
  241.5 4.9 collective-permute-start.5
  287.1 11.6 %all-to-all-start = ((s32[8,1,128]{2,1,0:T(1,128)}), s32[8,1,128]{2,1,0:T(1,128)S(1)}, u32[]{:S(2)}, u32[]{:S(2)}) async-start(s32[8,1,128]{2,1,0:T(1,128)} %bitcast.27), calls=%async_computation | async-start | bytes 8192 | tf_op jit(solution)/shard_map/all_to_all | solution.py:114
  308.0 10.1 %all-to-all-start.1 = ((bf16[8,128,96]{1,2,0:T(8,128)(2,1)}), bf16[8,128,96]{1,2,0:T(8,128)(2,1)S(1)}, u32[]{:S(2)}, u32[]{:S(2)}) async-start(bf16[8,128,96]{1,2,0:T(8,128)(2,1)} %copy.95), calls=%async_computation.1 | async-start | bytes 393216 | tf_op jit(solution)/shard_map/all_to_all | solution.py:116
  339.5 10.8 %all-to-all-start.2 = ((bf16[8,128,96]{1,2,0:T(8,128)(2,1)}), bf16[8,128,96]{1,2,0:T(8,128)(2,1)}, u32[]{:S(2)}, u32[]{:S(2)}) async-start(bf16[8,128,96]{1,2,0:T(8,128)(2,1)} %copy.101), calls=%async_computation.2 | async-start | bytes 393216 | tf_op jit(solution)/shard_map/all_to_all | solution.py:133
  343.5 95.8 %reduce-scatter.4.cloned.1.call-start = ((), (), s32[]{:S(2)}) async-start(), calls=%async_computation.9 | async-start | bytes 1671168 | tf_op jit(solution)/shard_map/reduce_scatter | solution.py:151
  357.8 5.6 collective-permute-start.7
  362.1 3.6 collective-permute-start.6
  367.5 111.8 %copy-start.21 = (f32[512]{0:T(512)S(1)}, f32[512]{0:T(512)}, u32[]{:S(2)}) copy-start(f32[512]{0:T(512)} %get-tuple-element.41) | copy-start | bytes 6148
  367.5 195.7 %reduce-scatter.6.cloned.1.call-start = ((), (), s32[]{:S(2)}) async-start(), calls=%async_computation.10 | async-start | bytes 1671168 | tf_op jit(solution)/shard_map/reduce_scatter | solution.py:151
  480.6 4.3 collective-permute-start.9
  483.5 4.9 collective-permute-start.8
  490.2 184.4 %all-reduce.3.cloned.1.call-start = ((), (), s32[]{:S(2)}) async-start(), calls=%async_computation.12 | async-start | bytes 5308416 | tf_op jit(solution)/shard_map/psum | solution.py:166
  496.8 106.5 %copy-start.20 = (f32[512]{0:T(512)S(1)}, f32[512]{0:T(512)}, u32[]{:S(2)}) copy-start(f32[512]{0:T(512)} %get-tuple-element.39) | copy-start | bytes 6148
  610.1 141.8 %reduce-scatter.8.cloned.1.call-start = ((), (), s32[]{:S(2)}) async-start(), calls=%async_computation.11 | async-start | bytes 1671168 | tf_op jit(solution)/shard_map/reduce_scatter | solution.py:151
  610.3 3.2 collective-permute-start.11
  612.2 4.9 collective-permute-start.10
  674.7 78.5 %copy-start.29 = (f32[96]{0:T(128)S(1)}, f32[96]{0:T(128)}, u32[]{:S(2)}) copy-start(f32[96]{0:T(128)} %get-tuple-element.4) | copy-start | bytes 1156
  674.7 130.4 %copy-start.13 = (f32[96,512]{1,0:T(8,128)S(1)}, f32[96,512]{1,0:T(8,128)}, u32[]{:S(2)}) copy-start(f32[96,512]{1,0:T(8,128)} %get-tuple-element.14) | copy-start | bytes 589828
  674.7 130.4 %copy-start.19 = (f32[512]{0:T(512)S(1)}, f32[512]{0:T(512)}, u32[]{:S(2)}) copy-start(f32[512]{0:T(512)} %get-tuple-element.37) | copy-start | bytes 6148
  (25 other events, 671.0 us)
Sparse Core Ops, SparseCore 0:
  59.5 43.5 all-gather.5
  154.2 42.8 all-gather.7
  247.3 42.8 all-gather.9
  367.6 71.6 reduce-scatter.3
  490.4 72.8 reduce-scatter.5
  610.2 64.3 all-reduce.2
  677.9 73.9 reduce-scatter.7
